TPU v7x, 128 devices: a whole 4x4x4 slice. The times are simulated.
128 devices in a mesh: region: 16 (over y_lo, z, core), head: 8 (over y_hi, x).
Axes of the slice: x: 4, y: 4 (y_hi: 2, y_lo: 2; y = y_hi * 2 + y_lo), z: 4, core: 2. Of those that a mesh axis runs over, the one named last changes fastest.
Arguments:
- fine_tokens: float32 [73728, 512], P(('region', 'head')), may hold values from -6 to 6
- fine_shift: int32 [1], replicated, may hold values from 1 to 143
- window_counts: int32 [128], P('region'), may hold values from 36 to 144
- fine_qkv: bfloat16 [512, 1536], replicated, may hold values from -4 to 4
- fine_proj: bfloat16 [512, 512], replicated, may hold values from -0.25 to 0.25
- fine_up: bfloat16 [512, 2048], replicated, may hold values from -0.25 to 0.25
- fine_down: bfloat16 [2048, 512], replicated, may hold values from -0.125 to 0.125
- merge_weight: bfloat16 [2048, 1024], replicated, may hold values from -0.125 to 0.125
- coarse_qkv: bfloat16 [1024, 3072], P('region', 'head'), may hold values from -4 to 4
- coarse_proj: bfloat16 [1024, 1024], P('head', 'region'), may hold values from -0.1875 to 0.1875
- coarse_up: bfloat16 [1024, 4096], P('region', 'head'), may hold values from -0.1875 to 0.1875
- coarse_down: bfloat16 [4096, 1024], P('head', 'region'), may hold values from -0.09375 to 0.09375
- expand_weight: bfloat16 [1024, 2048], replicated, may hold values from -0.1875 to 0.1875
- out_weight: bfloat16 [1024, 512], replicated, may hold values from -0.1875 to 0.1875
Outputs:
- fine_result: float32 [73728, 512], P(('region', 'head'))
All inputs are finite; a program needn't handle non-finite values.
Results may differ from a plain program's by a relative error of at most 0.012.
Values may be sent and summed in bfloat16 or wider, within the bound.
No kernel may reach another device: no remote copies, remote signals or barrier semaphores. Data moves between devices by JAX's collectives and lax.ppermute only.
A program may use at most 128 MiB of HBM per device.

v0:
```python
import jax
import jax.numpy as jnp
from jax import lax
from jax.sharding import PartitionSpec as P

C = 512
HD = 64
HF = 8
HC = 16
WIN = 144


def with_halo(value, sides, width):
    edges = {}
    for axis, dim in sides:
        devices, length = (lax.axis_size(axis), value.shape[dim])
        up = [(i, (i + 1) % devices) for i in range(devices)]
        last = lax.slice_in_dim(value, length - width, length, axis=dim)
        initial = lax.slice_in_dim(value, 0, width, axis=dim)
        edges[dim] = (
            lax.ppermute(last, axis, up),
            lax.ppermute(initial, axis, [(b, a) for a, b in up]),
        )
    done = []
    for _, dim in sides:
        low, high = edges[dim]
        around = [(width, width) if d in done else (0, 0) for d in range(value.ndim)]
        value = jnp.concatenate([jnp.pad(low, around), value, jnp.pad(high, around)], axis=dim)
        done.append(dim)
    return value


def from_everyone(value, axis):
    devices = lax.axis_size(axis)
    return lax.all_to_all(
        jnp.broadcast_to(value[None], (devices, *value.shape)), axis, 0, 0, tiled=True
    )


def laid_out(blocks, dim):
    blocks = jnp.moveaxis(blocks, 0, dim)
    shape = blocks.shape
    return blocks.reshape(*shape[:dim], shape[dim] * shape[dim + 1], *shape[dim + 2 :])


def gathered_copies(value, axis, dim):
    blocks = from_everyone(value, axis)
    return laid_out(blocks, dim)


def turned_gather(arrays, axis, dims):
    turned = [jnp.moveaxis(a, dim, 0) for a, dim in zip(arrays, dims)]
    both = jnp.concatenate([t.reshape(len(t), -1) for t in turned], axis=1)
    filled, at, gathered = (lax.all_gather(both, axis, axis=0, tiled=True), 0, [])
    for t, dim in zip(turned, dims):
        share = filled[:, at : at + t[0].size].reshape(-1, *t.shape[1:])
        gathered.append(jnp.moveaxis(share, 0, dim))
        at += t[0].size
    return tuple(gathered)


def layer_norm(values):
    average = jnp.mean(values, axis=-1, keepdims=True)
    centred = values - average
    spread = jnp.mean(centred * centred, axis=-1, keepdims=True)
    return centred * lax.rsqrt(spread + 1e-05)


def window_attention(normed, qkv_weight, proj_weight, head_count, head_size, window, counts):
    row_count = normed.shape[0]
    window_total = row_count // window
    weight_heads = qkv_weight.reshape(qkv_weight.shape[0], head_count, 3 * head_size)
    packed = jnp.einsum(
        "nc,chj->hnj", normed, weight_heads, preferred_element_type=jnp.float32
    ).astype(jnp.bfloat16)
    packed = packed.reshape(head_count, window_total, window, 3 * head_size)
    queries = packed[..., :head_size]
    key_part = packed[..., head_size : 2 * head_size]
    value_part = packed[..., 2 * head_size :]
    scores = jnp.einsum(
        "hwqd,hwkd->hwqk", queries, key_part, preferred_element_type=jnp.float32
    ) * head_size ** (-0.5)
    if counts is not None:
        position = jnp.arange(window, dtype=jnp.int32)
        visible = position[None, :] < counts[:, None]
        scores = jnp.where(visible[None, :, None, :], scores, -1e30)
    row_max = jnp.max(scores, axis=-1, keepdims=True)
    raised = jnp.exp(scores - row_max)
    weights = (raised / jnp.sum(raised, axis=-1, keepdims=True)).astype(jnp.bfloat16)
    blended = jnp.einsum(
        "hwqk,hwkd->hwqd", weights, value_part, preferred_element_type=jnp.float32
    ).astype(jnp.bfloat16)
    blended = blended.reshape(head_count, row_count, head_size)
    proj_heads = proj_weight.reshape(head_count, head_size, proj_weight.shape[1])
    return jnp.einsum("hnd,hdc->nc", blended, proj_heads, preferred_element_type=jnp.float32)


def hidden_layer(normed, up_weight):
    hidden = jnp.dot(normed, up_weight, preferred_element_type=jnp.float32)
    return jax.nn.gelu(hidden, approximate=False).astype(jnp.bfloat16)


def body(
    fine_tokens,
    fine_shift,
    window_counts,
    fine_qkv,
    fine_proj,
    fine_up,
    fine_down,
    merge_weight,
    coarse_qkv,
    coarse_proj,
    coarse_up,
    coarse_down,
    expand_weight,
    out_weight,
):
    offset = fine_shift[0]
    local_rows = fine_tokens.shape[0]
    normed = layer_norm(fine_tokens).astype(jnp.bfloat16)
    extended = with_halo(normed, ((("region", "head"), 0),), WIN)
    rolled = lax.dynamic_slice_in_dim(extended, offset, local_rows + WIN, 0)
    attended = window_attention(rolled, fine_qkv, fine_proj, HF, HD, WIN, None)
    restored = lax.dynamic_slice_in_dim(attended, WIN - offset, local_rows, 0)
    fine_mid = fine_tokens + restored
    fine_hidden = hidden_layer(layer_norm(fine_mid).astype(jnp.bfloat16), fine_up)
    fine_out = fine_mid + jnp.dot(fine_hidden, fine_down, preferred_element_type=jnp.float32)
    merged = fine_out.reshape(local_rows // 4, 4 * C)
    grouped = layer_norm(merged).astype(jnp.bfloat16)
    coarse = jnp.dot(grouped, merge_weight, preferred_element_type=jnp.float32)
    coarse_norm = layer_norm(coarse).astype(jnp.bfloat16)
    weight_parts = (coarse_qkv, coarse_proj, coarse_up, coarse_down)
    columns = (
        gathered_copies(weight_parts[0], "head", 1),
        gathered_copies(weight_parts[1], "head", 0),
        gathered_copies(weight_parts[2], "head", 1),
        gathered_copies(weight_parts[3], "head", 0),
    )
    qkv_full, proj_full, up_full, down_full = turned_gather(
        (columns[0], columns[1], columns[2], columns[3]), "region", (0, 1, 0, 1)
    )
    window_total = coarse_norm.shape[0] // WIN
    own_counts = lax.dynamic_slice_in_dim(
        window_counts, lax.axis_index("head") * window_total, window_total, 0
    )
    coarse_mid = coarse + window_attention(
        coarse_norm, qkv_full, proj_full, HC, HD, WIN, own_counts
    )
    coarse_hidden = hidden_layer(layer_norm(coarse_mid).astype(jnp.bfloat16), up_full)
    coarse_out = coarse_mid + jnp.dot(coarse_hidden, down_full, preferred_element_type=jnp.float32)
    expanded = jnp.dot(
        coarse_out.astype(jnp.bfloat16), expand_weight, preferred_element_type=jnp.float32
    ).astype(jnp.bfloat16)
    spread_rows = expanded.reshape(local_rows, C)
    joined = jnp.concatenate([fine_out.astype(jnp.bfloat16), spread_rows], axis=1)
    return jnp.dot(joined, out_weight, preferred_element_type=jnp.float32)


def solution(mesh):
    in_specs = (
        P(("region", "head"), None),
        P(),
        P("region"),
        P(),
        P(),
        P(),
        P(),
        P(),
        P("region", "head"),
        P("head", "region"),
        P("region", "head"),
        P("head", "region"),
        P(),
        P(),
    )
    out_specs = P(("region", "head"), None)
    return jax.shard_map(body, mesh=mesh, in_specs=in_specs, out_specs=out_specs, check_vma=False)
```

profile of v0, /device:TPU:23, one launch (start us, length us, event | category | flops | bytes accessed | tf_op | source)
XLA Modules:
  0.0 256.5 jit_solution(4802875899977580490)
XLA Ops:
  6.5 0.9 broadcast_in_dim.18
  7.4 9.6 %all_to_all.20 = bf16[8,128,64]{1,2,0:T(8,128)(2,1)} all-to-all(bf16[8,128,64]{1,2,0:T(8,128)(2,1)S(1)} %broadcast_in_dim.18), channel_id=1, replica_groups=mesh['region'=16,'head'=8] {'head'}, dimensions={0} | all-to-all | bytes 262144 | tf_op jit(solution)/shard_map/all_to_all | solution.py:35
  17.0 0.8 broadcast_in_dim.17
  17.8 10.8 %all_to_all.21 = bf16[8,64,384]{2,1,0:T(8,128)(2,1)S(1)} all-to-all(bf16[8,64,384]{2,1,0:T(8,128)(2,1)S(1)} %broadcast_in_dim.17), channel_id=1, replica_groups=mesh['region'=16,'head'=8] {'head'}, dimensions={0} | all-to-all | bytes 786432 | tf_op jit(solution)/shard_map/all_to_all | solution.py:35
  28.6 0.9 broadcast_in_dim.20
  29.5 12.0 %all_to_all.22 = bf16[8,512,64]{1,2,0:T(8,128)(2,1)S(1)} all-to-all(bf16[8,512,64]{1,2,0:T(8,128)(2,1)S(1)} %broadcast_in_dim.20), channel_id=1, replica_groups=mesh['region'=16,'head'=8] {'head'}, dimensions={0} | all-to-all | bytes 1048576 | tf_op jit(solution)/shard_map/all_to_all | solution.py:35
  41.5 0.8 broadcast_in_dim.19
  42.3 7.1 %all-to-all-start.2 = ((bf16[8,64,512]{2,1,0:T(8,128)(2,1)}), bf16[8,64,512]{2,1,0:T(8,128)(2,1)S(1)}, u32[]{:S(2)}, u32[]{:S(2)}) async-start(bf16[8,64,512]{2,1,0:T(8,128)(2,1)} %broadcast_in_dim.19), calls=%async_computation.2 | async-start | bytes 1048576 | tf_op jit(solution)/shard_map/all_to_all | solution.py:35
  49.4 1.6 bitcast_bitcast_fusion
  51.0 0.8 copy.81
  51.8 0.8 copy.84
  52.7 1.9 all-to-all-done.2
  54.6 2.5 pad_maximum_fusion
  57.4 0.3 multiply_reduce_fusion.3
  57.9 0.8 copy-done.6
  58.7 0.7 fusion.181
  59.4 10.6 %collective-permute-start = (bf16[144,512]{1,0:T(8,128)(2,1)}, bf16[144,512]{1,0:T(8,128)(2,1)}, u32[]{:S(2)}, u32[]{:S(2)}) collective-permute-start(bf16[144,512]{1,0:T(8,128)(2,1)} %get-tuple-element.10), channel_id=1, source_target_pairs={{0,1},{1,2},{2,3},{3,4},{4,5},{5,6},{6,7},{7,8},{8,9},{9,10},{10,1... | collective-permute-start | bytes 442376 | tf_op jit(solution)/shard_map/ppermute | solution.py:21
  70.7 0.6 dynamic_slice.11
  71.3 0.6 iota_compare_fusion
  72.0 0.5 collective-permute-done
  72.5 6.9 %collective-permute-done.1 = bf16[144,512]{1,0:T(8,128)(2,1)} collective-permute-done((bf16[144,512]{1,0:T(8,128)(2,1)S(1)}, bf16[144,512]{1,0:T(8,128)(2,1)}, u32[]{:S(2)}, u32[]{:S(2)}) %collective-permute-start.1) | collective-permute-done | bytes 147488 | tf_op jit(solution)/shard_map/ppermute | solution.py:22
  79.3 3.3 %fusion.94 = f32[720,1536]{0,1:S(1)} fusion(bf16[512,1536]{1,0:T(8,128)(2,1)} %param.17, s32[]{:T(128)S(6)} %select_n.14, bf16[144,512]{1,0:T(8,128)(2,1)} %collective-permute-done, bf16[576,512]{1,0:T(8,128)(2,1)} %copy-done.6, bf16[144,512]{1,0:T(8,128)(2,1)} %collective-permute-done.1), kind=kOutput, calls=%fused_computation.122 | convolution fusion | flops 1134673920 | bytes 7176196
  82.6 1.7 convert_bitcast_fusion
  84.4 4.5 %copy.55 = bf16[8,720,192]{2,1,0:T(8,128)(2,1)} copy(bf16[8,720,192]{1,2,0:T(8,128)(2,1)} %convert_bitcast_fusion) | data formatting | bytes 4423680 | tf_op jit(solution)/shard_map/convert_element_type | solution.py:75
  88.9 2.9 %fusion.35 = f32[8,5,144,144]{2,3,1,0:T(8,128)S(1)} fusion(bf16[8,5,144,192]{3,2,1,0:T(8,128)(2,1)} %bitcast.89), kind=kOutput, calls=%fused_computation.61 | convolution fusion | flops 106168320 | bytes 5529600 | tf_op jit(solution)/shard_map/hwqd,hwkd->hwqk/dot_general | solution.py:80
  91.8 5.6 %fusion.182 = (f32[8,5,144]{2,1,0:T(8,128)S(1)}, f32[8,5,144,144]{2,3,1,0:T(8,128)S(1)}) fusion(f32[8,5,144,144]{2,3,1,0:T(8,128)S(1)} %fusion.35), kind=kOutput, calls=%fused_computation.223 | output fusion | flops 3317903 | bytes 6658560 | tf_op jit(solution)/shard_map/sub | solution.py:88
  97.5 1.9 fusion.34
  99.4 2.7 %copy.60 = bf16[8,5,144,64]{3,2,1,0:T(8,128)(2,1)} copy(bf16[8,5,144,64]{2,3,1,0:T(8,128)(2,1)} %fusion.34) | data formatting | bytes 1474560 | tf_op jit(solution)/shard_map/convert_element_type | solution.py:92
  102.0 2.2 convolution_bitcast_fusion
  104.3 0.3 fusion.179
  104.6 1.0 copy-done.4
  105.6 0.3 multiply_reduce_fusion.2
  105.9 14.3 %fusion.183 = (f32[576]{0:T(1024)S(1)}, f32[576,512]{1,0:T(8,128)S(1)}) fusion(f32[576,512]{1,0:T(8,128)} %copy-done.4, bf16[2048,512]{1,0:T(8,128)(2,1)S(1)} %copy-done, bf16[512,2048]{1,0:T(8,128)(2,1)} %param.19, f32[576]{0:T(1024)S(1)} %add_rsqrt_fusion, f32[576]{0:T(1024)S(1)} %broadcast_multiply_fusion), kind=kOutput, calls=%fused_computation.224 | convolution fusion | flops 2494070272 | bytes 6560512 | tf_op jit(solution)/shard_map/dot_general | solution.py:128
  120.6 0.5 reshape.155
  121.2 1.1 fusion.180
  122.5 3.3 %fusion.184 = (f32[144]{0:T(256)S(1)}, f32[144,1024]{1,0:T(8,128)S(1)}) fusion(bf16[2048,1024]{1,0:T(8,128)(2,1)} %param.21, f32[144,2048]{1,0:T(8,128)S(1)} %reshape.155, f32[144]{0:T(256)S(1)} %add_rsqrt_fusion.4, f32[144]{0:T(256)S(1)} %broadcast_multiply_fusion.4), kind=kOutput, calls=%fused_computation.225 | convolution fusion | flops 605011840 | bytes 5965504 | tf_op jit(solution)/shard_map/dot_general | solution.py:131
  126.0 71.1 %all-gather.2.cloned.1.call-done = bf16[1024,12288]{1,0:T(8,128)(2,1)} async-done(((bf16[64,12288]{1,0:T(8,128)(2,1)}), bf16[1024,12288]{1,0:T(8,128)(2,1)}) %all-gather.2.cloned.1.call-update) | async-done | bytes 25165840 | tf_op jit(solution)/shard_map/all_gather | solution.py:54
  197.2 5.9 %slice.53 = bf16[1024,3072]{1,0:T(8,128)(2,1)} slice(bf16[1024,12288]{1,0:T(8,128)(2,1)} %all-gather.2.cloned.1.call-done), slice={[0:1024], [0:3072]} | slice | bytes 12582912 | tf_op jit(solution)/shard_map/slice | solution.py:56
  203.1 8.6 %copy.66 = bf16[1024,3072]{0,1:T(8,128)(2,1)} copy(bf16[1024,3072]{1,0:T(8,128)(2,1)} %slice.53) | data formatting | bytes 12582912 | tf_op jit(solution)/shard_map/slice | solution.py:56
  211.7 1.8 slice_bitcast_fusion
  213.5 2.6 %copy.71 = bf16[1024,1024]{1,0:T(8,128)(2,1)} copy(bf16[1024,1024]{0,1:T(8,128)(2,1)S(1)} %slice_bitcast_fusion) | data formatting | bytes 4194304 | tf_op jit(solution)/shard_map/transpose | solution.py:57
  216.0 6.2 %fusion.39 = bf16[16,1,144,192]{3,2,0,1:T(8,128)(2,1)} fusion(bf16[1024,16,192]{0,2,1:T(8,128)(2,1)} %bitcast.91, f32[144,1024]{1,0:T(8,128)S(1)} %get-tuple-element.16, f32[144]{0:T(256)S(1)} %add_rsqrt_fusion.3, f32[144]{0:T(256)S(1)} %broadcast_multiply_fusion.3), kind=kOutput, calls=%fused_computation.66 | convolution fusion | flops 906854400 | bytes 7767168 | tf_op jit(solution)/shard_map/nc,chj->hnj/dot_general | solution.py:73
  222.2 3.8 %fusion.185 = (f32[16,144]{1,0:T(8,128)S(1)}, f32[16,144,144]{1,2,0:T(8,128)}) fusion(pred[144]{0:T(512)(128)(4,1)S(1)} %iota_compare_fusion, bf16[16,1,144,192]{3,2,0,1:T(8,128)(2,1)} %fusion.39), kind=kOutput, calls=%fused_computation.226 | convolution fusion | flops 43794576 | bytes 2221200 | tf_op jit(solution)/shard_map/sub | solution.py:88
  226.1 2.7 %fusion.186 = (f32[144]{0:T(256)S(1)}, f32[144,1024]{1,0:T(8,128)S(1)}) fusion(f32[144,1024]{1,0:T(8,128)S(1)} %get-tuple-element.16, bf16[16,64,1024]{2,1,0:T(8,128)(2,1)S(1)} %bitcast.93, f32[16,144,144]{1,2,0:T(8,128)} %get-tuple-element.18, f32[16,144]{1,0:T(8,128)S(1)} %get-tuple-element.17, bf16[16,1,144,192]{3,2,0,1:T(8,128)(2,1)} %fusion.39), kind=kOutput, calls=%fused_computation.227 | convolution fusion | flops 345563008 | bytes 6235712 | tf_op jit(solution)/shard_map/hnd,hdc->nc/dot_general | solution.py:95
  229.0 13.2 %fusion.47 = bf16[144,1024]{1,0:T(8,128)(2,1)S(1)} fusion(f32[144,1024]{1,0:T(8,128)S(1)} %get-tuple-element.20, bf16[1024,12288]{1,0:T(8,128)(2,1)} %all-gather.2.cloned.1.call-done, f32[144]{0:T(256)S(1)} %add_rsqrt_fusion.2, f32[144]{0:T(256)S(1)} %broadcast_multiply_fusion.2), kind=kOutput, calls=%fused_computation.72 | convolution fusion | flops 2454994944 | bytes 18253824 | tf_op jit(solution)/shard_map/dot_general | solution.py:151
  242.2 3.0 %convolution_convert_fusion = bf16[144,2048]{1,0:T(8,128)(2,1)S(1)} fusion(bf16[144,1024]{1,0:T(8,128)(2,1)S(1)} %fusion.47, bf16[1024,2048]{1,0:T(8,128)(2,1)} %param.26), kind=kOutput, calls=%fused_computation.32 | convolution fusion | flops 604274688 | bytes 5079040 | tf_op jit(solution)/shard_map/dot_general | solution.py:152
  245.3 1.2 reshape.166
  246.4 3.2 %fusion.55 = f32[576,512]{1,0:T(8,128)} fusion(bf16[1024,512]{1,0:T(8,128)(2,1)} %param.27, bf16[576,512]{1,0:T(8,128)(2,1)} %reshape.166, bf16[576,512]{1,0:T(8,128)(2,1)S(1)} %copy-done.7), kind=kOutput, calls=%fused_computation.73 | convolution fusion | flops 606339072 | bytes 3407872 | tf_op jit(solution)/shard_map/dot_general | solution.py:157
  (42 shorter events, 1.6 us)
Async XLA Ops:
  6.5 99.4 %copy-start = (bf16[2048,512]{1,0:T(8,128)(2,1)S(1)}, bf16[2048,512]{1,0:T(8,128)(2,1)}, u32[]{:S(2)}) copy-start(bf16[2048,512]{1,0:T(8,128)(2,1)} %param.20) | copy-start | bytes 6291460
  6.5 34.9 %copy-start.8 = (bf16[64,512]{1,0:T(8,128)(2,1)S(1)}, bf16[64,512]{1,0:T(8,128)(2,1)}, u32[]{:S(2)}) copy-start(bf16[64,512]{1,0:T(8,128)(2,1)} %param.24) | copy-start | bytes 196612
  42.3 12.3 %all-to-all-start.2 = ((bf16[8,64,512]{2,1,0:T(8,128)(2,1)}), bf16[8,64,512]{2,1,0:T(8,128)(2,1)S(1)}, u32[]{:S(2)}, u32[]{:S(2)}) async-start(bf16[8,64,512]{2,1,0:T(8,128)(2,1)} %broadcast_in_dim.19), calls=%async_computation.2 | async-start | bytes 1048576 | tf_op jit(solution)/shard_map/all_to_all | solution.py:35
  49.4 147.7 %all-gather.2.cloned.1.call-start = ((), (), s32[]{:S(2)}) async-start(), calls=%async_computation.4 | async-start | bytes 26738688 | tf_op jit(solution)/shard_map/all_gather | solution.py:54
  54.6 2.6 %copy-start.2 = (f32[576,512]{1,0:T(8,128)S(1)}, f32[576,512]{1,0:T(8,128)}, u32[]{:S(2)}) copy-start(f32[576,512]{1,0:T(8,128)} %param.14) | copy-start | bytes 3538948
  57.2 13.5 %copy-start.9 = (s32[8]{0:T(128)S(1)}, s32[8]{0:T(128)}, u32[]{:S(2)}) copy-start(s32[8]{0:T(128)} %param.16) | copy-start | bytes 100
  57.9 0.8 copy-start.6
  59.4 13.0 %collective-permute-start = (bf16[144,512]{1,0:T(8,128)(2,1)}, bf16[144,512]{1,0:T(8,128)(2,1)}, u32[]{:S(2)}, u32[]{:S(2)}) collective-permute-start(bf16[144,512]{1,0:T(8,128)(2,1)} %get-tuple-element.10), channel_id=1, source_target_pairs={{0,1},{1,2},{2,3},{3,4},{4,5},{5,6},{6,7},{7,8},{8,9},{9,10},{10,1... | collective-permute-start | bytes 442376 | tf_op jit(solution)/shard_map/ppermute | solution.py:21
  70.0 9.3 %collective-permute-start.1 = (bf16[144,512]{1,0:T(8,128)(2,1)S(1)}, bf16[144,512]{1,0:T(8,128)(2,1)}, u32[]{:S(2)}, u32[]{:S(2)}) collective-permute-start(bf16[144,512]{1,0:T(8,128)(2,1)S(1)} %get-tuple-element.9), channel_id=1, source_target_pairs={{1,0},{2,1},{3,2},{4,3},{5,4},{6,5},{7,6},{8,7},{9,8},{10,9},{11,1... | collective-permute-start | bytes 442376 | tf_op jit(solution)/shard_map/ppermute | solution.py:22
  91.8 5.6 %copy-start.3 = (bf16[8,720,192]{2,1,0:T(8,128)(2,1)S(1)}, bf16[8,720,192]{2,1,0:T(8,128)(2,1)}, u32[]{:S(2)}) copy-start(bf16[8,720,192]{2,1,0:T(8,128)(2,1)} %copy.55) | copy-start | bytes 6635524
  104.6 1.0 copy-start.4
  222.2 3.8 %copy-start.5 = (bf16[1024,1024]{1,0:T(8,128)(2,1)S(1)}, bf16[1024,1024]{1,0:T(8,128)(2,1)}, u32[]{:S(2)}) copy-start(bf16[1024,1024]{1,0:T(8,128)(2,1)} %copy.71) | copy-start | bytes 6291460
  242.2 4.2 %copy-start.7 = (bf16[576,512]{1,0:T(8,128)(2,1)S(1)}, bf16[576,512]{1,0:T(8,128)(2,1)}, u32[]{:S(2)}) copy-start(bf16[576,512]{1,0:T(8,128)(2,1)} %get-tuple-element.7) | copy-start | bytes 1769476
  245.3 4.4 %copy-start.1 = (bf16[2048,512]{1,0:T(8,128)(2,1)S(1)}, bf16[2048,512]{1,0:T(8,128)(2,1)}, u32[]{:S(2)}) copy-start(bf16[2048,512]{1,0:T(8,128)(2,1)} %param.20) | copy-start | bytes 6291460
Sparse Core Ops, SparseCore 0:
  57.3 139.8 all-gather.1
where the time goes:
time: 258 us; the launch traced here: 256 us
  waiting for transfers between devices  80.4 us (31%)
  matrix products  60.1 us (23%)
  local copies, waits for them, and re-layouts  38 us (15%)
  blocking collectives  32.3 us (13%)
  starting transfers between devices  17.8 us (7%)
  between operations  14.3 us (6%)
  other arithmetic  13.6 us (5%)
    all_gather x1, waiting for transfers between devices, turned_gather(): lax.all_gather(both, axis, axis=0, tiled=True)  71.1 us
    all_to_all x3, blocking collectives, from_everyone(): lax.all_to_all(jnp.broadcast_to(value[None], (devices, *value.shape)), ax...  32.3 us
    slice x2, local copies, waits for them, and re-layouts, turned_gather(): share = filled[:, at:at + t[0].size].reshape(-1, *t.shape[1:])  14.5 us
    dot_general x1, matrix products, body(): jnp.dot(fine_hidden, fine_down, preferred_element_type=jnp.float32)  14.3 us
    dot_general x1, matrix products, body(): jnp.dot(coarse_hidden, down_full, preferred_element_type=jnp.float32)  13.2 us
    ppermute x1, starting transfers between devices, with_halo(): lax.ppermute(last, axis, up)  10.6 us
    all_to_all x1, starting transfers between devices, from_everyone(): lax.all_to_all(jnp.broadcast_to(value[None], (devices, *value.shape)), ax...  7.13 us
    ppermute x1, waiting for transfers between devices, with_halo(): lax.ppermute(initial, axis, [(b, a) for a, b in up])  6.87 us
  transfers between devices with their start and end apart: 4, of which 4 were waited for; matrix products, arithmetic and copies ran while one was open for 20% of the time, Pallas kernels for 0%

commit v1 on v0

--- a/solution.py
+++ b/solution.py
@@ -51,7 +51,13 @@
 def turned_gather(arrays, axis, dims):
     turned = [jnp.moveaxis(a, dim, 0) for a, dim in zip(arrays, dims)]
     both = jnp.concatenate([t.reshape(len(t), -1) for t in turned], axis=1)
-    filled, at, gathered = (lax.all_gather(both, axis, axis=0, tiled=True), 0, [])
+    filled, at, gathered = (
+        jnp.concatenate(
+            lax.all_to_all(jnp.stack([both] * lax.axis_size(axis)), axis, 0, 0), axis=0
+        ),
+        0,
+        [],
+    )
     for t, dim in zip(turned, dims):
         share = filled[:, at : at + t[0].size].reshape(-1, *t.shape[1:])
         gathered.append(jnp.moveaxis(share, 0, dim))

time: 258 us -> 524 us (2.03); the launches traced: 256 us -> 514 us
  waiting for transfers between devices: 80.4 us -> 339 us
  between operations: 14.3 us -> 0.95 us
  local copies, waits for them, and re-layouts: 38 us -> 46.6 us
  starting transfers between devices: 17.8 us -> 23.4 us
    all_to_all x0 -> x1, waiting for transfers between devices: none -> 329 us  [turned_gather(): lax.all_to_all(jnp.stack([both] * lax.axis_size(axis)), axis, 0, 0)]
    all_gather x1 -> x0, waiting for transfers between devices: 71.1 us -> none  [turned_gather(): lax.all_gather(both, axis, axis=0, tiled=True)]
    all_to_all x0 -> x1, starting transfers between devices: none -> 11.6 us  [turned_gather(): lax.all_to_all(jnp.stack([both] * lax.axis_size(axis)), axis, 0, 0)]
    another operation x0 -> x1, local copies, waits for them, and re-layouts: none -> 8.58 us  [turned_gather(): jnp.stack([both] * lax.axis_size(axis))]
    ppermute x1, starting transfers between devices: 10.6 us -> 4.66 us  [with_halo(): lax.ppermute(last, axis, up)]
  transfers between devices with their start and end apart: 4 -> 4, of which waited for: 4 -> 4; matrix products, arithmetic and copies ran while one was open for 20% -> 10% of each run, Pallas kernels for 0% -> 0%
where the time goes in v1:
time: 524 us; the launch traced here: 514 us
  waiting for transfers between devices  339 us (65%)
  matrix products  59.5 us (11%)
  local copies, waits for them, and re-layouts  46.6 us (9%)
  blocking collectives  32.3 us (6%)
  starting transfers between devices  23.4 us (4%)
  other arithmetic  12.2 us (2%)
    all_to_all x1, waiting for transfers between devices, turned_gather(): lax.all_to_all(jnp.stack([both] * lax.axis_size(axis)), axis, 0, 0)  329 us
    all_to_all x3, blocking collectives, from_everyone(): lax.all_to_all(jnp.broadcast_to(value[None], (devices, *value.shape)), ax...  32.3 us
    slice x2, local copies, waits for them, and re-layouts, turned_gather(): share = filled[:, at:at + t[0].size].reshape(-1, *t.shape[1:])  14.6 us
    dot_general x1, matrix products, body(): jnp.dot(fine_hidden, fine_down, preferred_element_type=jnp.float32)  14.1 us
    dot_general x1, matrix products, body(): jnp.dot(coarse_hidden, down_full, preferred_element_type=jnp.float32)  13.2 us
    all_to_all x1, starting transfers between devices, turned_gather(): lax.all_to_all(jnp.stack([both] * lax.axis_size(axis)), axis, 0, 0)  11.6 us
  transfers between devices with their start and end apart: 4, of which 4 were waited for; matrix products, arithmetic and copies ran while one was open for 10% of the time, Pallas kernels for 0%

profile of v1, /device:TPU:23, one launch (start us, length us, event | category | flops | bytes accessed | tf_op | source)
XLA Modules:
  0.0 514.3 jit_solution(17543340797690856212)
XLA Ops:
  0.0 0.9 broadcast_in_dim.18
  0.9 9.6 %all_to_all.25 = bf16[8,128,64]{1,2,0:T(8,128)(2,1)} all-to-all(bf16[8,128,64]{1,2,0:T(8,128)(2,1)S(1)} %broadcast_in_dim.18), channel_id=1, replica_groups=mesh['region'=16,'head'=8] {'head'}, dimensions={0} | all-to-all | bytes 262144 | tf_op jit(solution)/shard_map/all_to_all | solution.py:35
  10.5 0.8 broadcast_in_dim.17
  11.3 10.8 %all_to_all.26 = bf16[8,64,384]{2,1,0:T(8,128)(2,1)S(1)} all-to-all(bf16[8,64,384]{2,1,0:T(8,128)(2,1)S(1)} %broadcast_in_dim.17), channel_id=1, replica_groups=mesh['region'=16,'head'=8] {'head'}, dimensions={0} | all-to-all | bytes 786432 | tf_op jit(solution)/shard_map/all_to_all | solution.py:35
  22.1 0.9 broadcast_in_dim.20
  23.0 12.0 %all_to_all.27 = bf16[8,512,64]{1,2,0:T(8,128)(2,1)S(1)} all-to-all(bf16[8,512,64]{1,2,0:T(8,128)(2,1)S(1)} %broadcast_in_dim.20), channel_id=1, replica_groups=mesh['region'=16,'head'=8] {'head'}, dimensions={0} | all-to-all | bytes 1048576 | tf_op jit(solution)/shard_map/all_to_all | solution.py:35
  34.9 0.8 broadcast_in_dim.19
  35.8 7.1 %all-to-all-start.2 = ((bf16[8,64,512]{2,1,0:T(8,128)(2,1)}), bf16[8,64,512]{2,1,0:T(8,128)(2,1)S(1)}, u32[]{:S(2)}, u32[]{:S(2)}) async-start(bf16[8,64,512]{2,1,0:T(8,128)(2,1)} %broadcast_in_dim.19), calls=%async_computation.2 | async-start | bytes 1048576 | tf_op jit(solution)/shard_map/all_to_all | solution.py:35
  42.9 1.6 bitcast_bitcast_fusion
  44.5 0.8 copy.79
  45.3 0.8 copy.82
  46.1 1.9 all-to-all-done.2
  48.1 1.2 pad_maximum_fusion
  49.2 8.6 %stack.2 = bf16[16,64,12288]{2,1,0:T(8,128)(2,1)} broadcast(bf16[64,12288]{1,0:T(8,128)(2,1)S(1)} %pad_maximum_fusion), dimensions={1,2} | broadcast | bytes 26738688 | tf_op jit(solution)/shard_map/stack | solution.py:56
  57.8 11.6 %all-to-all-start.4 = ((bf16[16,64,12288]{2,1,0:T(8,128)(2,1)}), bf16[16,64,12288]{2,1,0:T(8,128)(2,1)}, u32[]{:S(2)}, u32[]{:S(2)}) async-start(bf16[16,64,12288]{2,1,0:T(8,128)(2,1)} %stack.2), calls=%async_computation.4 | async-start | bytes 50331648 | tf_op jit(solution)/shard_map/all_to_all | solution.py:56
  70.2 0.8 copy-done.7
  71.0 0.7 fusion.181
  71.7 4.7 collective-permute-start
  77.0 0.7 dynamic_slice.11
  77.7 0.7 iota_compare_fusion
  78.4 1.2 collective-permute-done
  79.6 7.4 %collective-permute-done.1 = bf16[144,512]{1,0:T(8,128)(2,1)} collective-permute-done((bf16[144,512]{1,0:T(8,128)(2,1)S(1)}, bf16[144,512]{1,0:T(8,128)(2,1)}, u32[]{:S(2)}, u32[]{:S(2)}) %collective-permute-start.1) | collective-permute-done | bytes 147488 | tf_op jit(solution)/shard_map/ppermute | solution.py:22
  87.0 3.3 fusion.94
  90.2 1.7 convert_bitcast_fusion
  91.9 4.5 copy.53
  96.4 2.9 fusion.35
  99.3 5.6 %fusion.182 = (f32[8,5,144]{2,1,0:T(8,128)S(1)}, f32[8,5,144,144]{2,3,1,0:T(8,128)S(1)}) fusion(f32[8,5,144,144]{2,3,1,0:T(8,128)S(1)} %fusion.35), kind=kOutput, calls=%fused_computation.223 | output fusion | flops 3317903 | bytes 6658560 | tf_op jit(solution)/shard_map/sub | solution.py:94
  105.0 1.9 fusion.34
  106.9 2.7 copy.58
  109.5 2.1 convolution_bitcast_fusion
  111.6 0.3 fusion.179
  111.9 1.0 copy-done.4
  113.2 14.1 %fusion.183 = (f32[576]{0:T(1024)S(1)}, f32[576,512]{1,0:T(8,128)S(1)}) fusion(f32[576,512]{1,0:T(8,128)} %copy-done.4, bf16[2048,512]{1,0:T(8,128)(2,1)S(1)} %copy-done, bf16[512,2048]{1,0:T(8,128)(2,1)} %param.19, f32[576]{0:T(1024)S(1)} %add_rsqrt_fusion, f32[576]{0:T(1024)S(1)} %broadcast_multiply_fusion), kind=kOutput, calls=%fused_computation.224 | convolution fusion | flops 2494070272 | bytes 6560512 | tf_op jit(solution)/shard_map/dot_general | solution.py:134
  127.3 0.5 reshape.160
  128.3 1.1 fusion.180
  129.6 3.1 fusion.184
  133.0 328.7 %all-to-all-done.4 = bf16[16,64,12288]{2,1,0:T(8,128)(2,1)} async-done(((bf16[16,64,12288]{2,1,0:T(8,128)(2,1)}), bf16[16,64,12288]{2,1,0:T(8,128)(2,1)}, u32[]{:S(2)}, u32[]{:S(2)}) %all-to-all-start.4) | async-done | bytes 25165856 | tf_op jit(solution)/shard_map/all_to_all | solution.py:56
  461.7 1.8 slice_bitcast_fusion
  463.5 5.9 %slice.53 = bf16[1024,3072]{1,0:T(8,128)(2,1)} slice(bf16[1024,12288]{1,0:T(8,128)(2,1)} %bitcast.14), slice={[0:1024], [0:3072]} | slice | bytes 12582912 | tf_op jit(solution)/shard_map/slice | solution.py:62
  469.4 2.5 copy.69
  472.0 8.7 %copy.64 = bf16[1024,3072]{0,1:T(8,128)(2,1)} copy(bf16[1024,3072]{1,0:T(8,128)(2,1)} %slice.53) | data formatting | bytes 12582912 | tf_op jit(solution)/shard_map/slice | solution.py:62
  480.7 6.2 %fusion.39 = bf16[16,1,144,192]{3,2,0,1:T(8,128)(2,1)} fusion(bf16[1024,16,192]{0,2,1:T(8,128)(2,1)} %bitcast.92, f32[144,1024]{1,0:T(8,128)S(1)} %get-tuple-element.16, f32[144]{0:T(256)S(1)} %add_rsqrt_fusion.3, f32[144]{0:T(256)S(1)} %broadcast_multiply_fusion.3), kind=kOutput, calls=%fused_computation.66 | convolution fusion | flops 906854400 | bytes 7767168 | tf_op jit(solution)/shard_map/nc,chj->hnj/dot_general | solution.py:79
  486.8 3.8 fusion.185
  490.7 2.7 fusion.186
  493.6 13.2 %fusion.47 = bf16[144,1024]{1,0:T(8,128)(2,1)S(1)} fusion(f32[144,1024]{1,0:T(8,128)S(1)} %get-tuple-element.20, bf16[1024,12288]{1,0:T(8,128)(2,1)} %bitcast.14, f32[144]{0:T(256)S(1)} %add_rsqrt_fusion.2, f32[144]{0:T(256)S(1)} %broadcast_multiply_fusion.2), kind=kOutput, calls=%fused_computation.72 | convolution fusion | flops 2454994944 | bytes 18253824 | tf_op jit(solution)/shard_map/dot_general | solution.py:157
  506.9 3.0 convolution_convert_fusion
  509.9 1.2 reshape.172
  511.1 3.2 fusion.55
  (44 shorter events, 2.2 us)
Async XLA Ops:
  0.0 113.2 %copy-start = (bf16[2048,512]{1,0:T(8,128)(2,1)S(1)}, bf16[2048,512]{1,0:T(8,128)(2,1)}, u32[]{:S(2)}) copy-start(bf16[2048,512]{1,0:T(8,128)(2,1)} %param.20) | copy-start | bytes 6291460
  0.0 34.9 %copy-start.9 = (bf16[64,512]{1,0:T(8,128)(2,1)S(1)}, bf16[64,512]{1,0:T(8,128)(2,1)}, u32[]{:S(2)}) copy-start(bf16[64,512]{1,0:T(8,128)(2,1)} %param.24) | copy-start | bytes 196612
  35.8 12.3 %all-to-all-start.2 = ((bf16[8,64,512]{2,1,0:T(8,128)(2,1)}), bf16[8,64,512]{2,1,0:T(8,128)(2,1)S(1)}, u32[]{:S(2)}, u32[]{:S(2)}) async-start(bf16[8,64,512]{2,1,0:T(8,128)(2,1)} %broadcast_in_dim.19), calls=%async_computation.2 | async-start | bytes 1048576 | tf_op jit(solution)/shard_map/all_to_all | solution.py:35
  45.3 2.8 copy-start.6
  57.8 11.6 %copy-start.2 = (f32[576,512]{1,0:T(8,128)S(1)}, f32[576,512]{1,0:T(8,128)}, u32[]{:S(2)}) copy-start(f32[576,512]{1,0:T(8,128)} %param.14) | copy-start | bytes 3538948
  57.8 403.9 %all-to-all-start.4 = ((bf16[16,64,12288]{2,1,0:T(8,128)(2,1)}), bf16[16,64,12288]{2,1,0:T(8,128)(2,1)}, u32[]{:S(2)}, u32[]{:S(2)}) async-start(bf16[16,64,12288]{2,1,0:T(8,128)(2,1)} %stack.2), calls=%async_computation.4 | async-start | bytes 50331648 | tf_op jit(solution)/shard_map/all_to_all | solution.py:56
  69.5 7.5 %copy-start.10 = (s32[8]{0:T(128)S(1)}, s32[8]{0:T(128)}, u32[]{:S(2)}) copy-start(s32[8]{0:T(128)} %param.16) | copy-start | bytes 100
  70.2 0.8 copy-start.7
  71.7 7.9 %collective-permute-start = (bf16[144,512]{1,0:T(8,128)(2,1)}, bf16[144,512]{1,0:T(8,128)(2,1)}, u32[]{:S(2)}, u32[]{:S(2)}) collective-permute-start(bf16[144,512]{1,0:T(8,128)(2,1)} %get-tuple-element.10), channel_id=1, source_target_pairs={{0,1},{1,2},{2,3},{3,4},{4,5},{5,6},{6,7},{7,8},{8,9},{9,10},{10,1... | collective-permute-start | bytes 442376 | tf_op jit(solution)/shard_map/ppermute | solution.py:21
  76.4 10.6 %collective-permute-start.1 = (bf16[144,512]{1,0:T(8,128)(2,1)S(1)}, bf16[144,512]{1,0:T(8,128)(2,1)}, u32[]{:S(2)}, u32[]{:S(2)}) collective-permute-start(bf16[144,512]{1,0:T(8,128)(2,1)S(1)} %get-tuple-element.9), channel_id=1, source_target_pairs={{1,0},{2,1},{3,2},{4,3},{5,4},{6,5},{7,6},{8,7},{9,8},{10,9},{11,1... | collective-permute-start | bytes 442376 | tf_op jit(solution)/shard_map/ppermute | solution.py:22
  99.3 5.6 %copy-start.3 = (bf16[8,720,192]{2,1,0:T(8,128)(2,1)S(1)}, bf16[8,720,192]{2,1,0:T(8,128)(2,1)}, u32[]{:S(2)}) copy-start(bf16[8,720,192]{2,1,0:T(8,128)(2,1)} %copy.53) | copy-start | bytes 6635524
  111.9 1.0 copy-start.4
  486.8 3.8 copy-start.5
  506.8 4.2 copy-start.8
  509.9 4.4 copy-start.1
